TPU v7x, 512 devices: a whole 4x4x16 slice. The times are simulated.
512 devices in a mesh: ex: 64 (over y_lo, z, core), hid: 8 (over x, y_hi).
Axes of the slice: x: 4, y: 4 (y_hi: 2, y_lo: 2; y = y_hi * 2 + y_lo), z: 16, core: 2. Of those that a mesh axis runs over, the one named last changes fastest.
Arguments:
- activations: bfloat16 [256, 192, 14336], P('ex', None, 'hid'), may hold values from -6 to 6
- out_grads: bfloat16 [256, 192, 4096], P('ex', None, 'hid'), may hold values from -6 to 6
- token_mask: int32 [256, 192], P('ex'), may hold values from 0 to 1, as said below
- proj_in: bfloat16 [14336, 64], P('hid'), may hold values from -0.046875 to 0.046875
- proj_out: bfloat16 [4096, 64], P('hid'), may hold values from -0.09375 to 0.09375
- inv_input: float32 [64, 64], replicated, as said below
- inv_output: float32 [64, 64], replicated, as said below
- query_feats: bfloat16 [4096, 4096], P('ex', 'hid'), may hold values from -6 to 6
Outputs:
- scores: float32 [4096, 256], P('ex', 'hid')
Inputs may be any that keep to these rules, and one draw needn't show every extreme that they name: `token_mask`: each row is 48 or more ones followed by zeros; some row is all ones. `inv_input`: symmetric. `inv_output`: symmetric.
All inputs are finite; a program needn't handle non-finite values.
Results may differ from a plain program's by a relative error of at most 0.0041.
Values may be sent and summed in bfloat16 or wider, within the bound.
A program may use at most 64 MiB of HBM per device.

v0:
```python
import jax
import jax.numpy as jnp
from jax import lax
from jax.sharding import PartitionSpec as P


def local(
    activations, out_grads, token_mask, proj_in, proj_out, inv_input, inv_output, query_feats
):
    seq_count, length, unit_local = activations.shape
    rank_width = proj_in.shape[1]
    hid_size = lax.axis_size("hid")
    row_block = rank_width // hid_size
    my_index = lax.axis_index("hid")
    in_part = jnp.dot(
        activations.reshape(seq_count * length, unit_local),
        proj_in,
        preferred_element_type=jnp.float32,
    )
    in_part = jnp.dot(in_part, inv_input, precision=lax.Precision.HIGHEST)
    out_part = jnp.dot(
        out_grads.reshape(seq_count * length, out_grads.shape[2]),
        proj_out,
        preferred_element_type=jnp.float32,
    )
    token_weight = token_mask.astype(jnp.float32)
    tok_count = jnp.sum(token_weight, axis=1)
    in_full, out_full = lax.psum((in_part, out_part), "hid")
    in_mine = lax.dynamic_slice_in_dim(in_full, my_index * row_block, row_block, 1)
    masked = in_mine.reshape(seq_count, length, row_block) * token_weight[:, :, None]
    outer = jnp.einsum(
        "slr,slq->srq",
        masked,
        out_full.reshape(seq_count, length, rank_width),
        precision=lax.Precision.HIGHEST,
    )
    train_feats = (
        (outer / tok_count[:, None, None])
        .astype(jnp.bfloat16)
        .reshape(seq_count, row_block * rank_width)
    )
    query_count = query_feats.shape[0]
    queries = query_feats.reshape(query_count, row_block, rank_width).astype(jnp.float32)
    query_pre = jnp.einsum("qij,jk->qik", queries, inv_output, precision=lax.Precision.HIGHEST)
    query_pre = query_pre.astype(jnp.bfloat16).reshape(query_count, row_block * rank_width)
    partial_value = jnp.einsum(
        "qk,tk->qt",
        query_pre,
        lax.all_gather(train_feats, "ex", axis=0, tiled=True),
        preferred_element_type=jnp.float32,
    )
    return lax.psum_scatter(partial_value, "hid", scatter_dimension=1, tiled=True)


def solution(mesh):
    return jax.shard_map(
        local,
        mesh=mesh,
        in_specs=(
            P("ex", None, "hid"),
            P("ex", None, "hid"),
            P("ex", None),
            P("hid", None),
            P("hid", None),
            P(),
            P(),
            P("ex", "hid"),
        ),
        out_specs=P("ex", "hid"),
        check_vma=False,
    )
```

profile of v0, /device:TPU:1, one launch (start us, length us, event | category | flops | bytes accessed | tf_op | source)
XLA Modules:
  0.0 264.1 jit_solution(6362297296101887833)
XLA Ops:
  6.5 0.0 copy-start
  6.5 0.0 all-reduce.3.cloned.1.call-start
  6.5 1.6 fusion.6
  8.2 0.2 reshape.28
  8.4 0.0 copy-start.3
  8.4 0.7 copy.17
  9.2 0.0 copy-done
  9.2 0.0 copy-start.4
  9.2 0.0 copy-start.1
  9.2 0.0 copy-start.2
  9.2 1.9 fusion.4
  11.1 0.0 copy-done.3
  11.1 1.0 fusion.5
  12.2 0.0 all-reduce.3.cloned.1.call-update
  12.2 0.0 reduce-scatter.2.cloned.1.call-start
  12.2 0.0 copy-done.4
  12.3 0.0 copy-done.1
  12.3 0.1 reshape.23
  12.4 0.0 copy-done.2
  12.4 0.2 convolution_convert_fusion
  12.7 0.1 copy.16
  12.8 0.1 reshape.24
  12.9 0.1 convert_reduce_fusion
  13.0 100.4 %all-reduce.3.cloned.1.call-done = (f32[4,192,64]{1,2,0:T(8,128)}, f32[768,64]{0,1:T(8,128)}) async-done(((f32[4,192,64]{1,2,0:T(8,128)}, f32[768,64]{0,1:T(8,128)}), (f32[4,192,64]{1,2,0:T(8,128)}, f32[768,64]{0,1:T(8,128)})) %all-reduce.3.cloned.1.call-update) | async-done | bytes 393232 | tf_op jit(solution)/shard_map/psum | solution.py:28
  113.4 0.7 constant_dynamic-slice_fusion
  114.1 0.1 reshape.26
  114.3 1.3 fusion
  115.5 0.1 reshape.30
  115.6 69.5 %all-gather = bf16[64,4,512]{2,1,0:T(4,128)(2,1)S(1)} all-gather(bf16[1,4,512]{2,1,0:T(4,128)(2,1)S(1)} %reshape.30), channel_id=1, replica_groups=mesh['ex'=64,'hid'=8] {'ex'}, dimensions={0}, use_global_device_ids=true | all-gather | bytes 266240 | tf_op jit(solution)/shard_map/all_gather | solution.py:49
  185.1 0.1 reshape.31
  185.1 0.9 fusion.7
  186.0 0.0 reduce-scatter.2.cloned.1.call-update
  186.0 71.2 %reduce-scatter.2.cloned.1.call-done = f32[64,32]{0,1:T(8,128)} async-done(((f32[64,256]{0,1:T(8,128)}), f32[64,32]{0,1:T(8,128)}) %reduce-scatter.2.cloned.1.call-update) | async-done | bytes 8208 | tf_op jit(solution)/shard_map/reduce_scatter | solution.py:52
  (3 shorter events, 0.0 us)
Async XLA Ops:
  6.5 2.6 copy-start
  6.5 106.9 %all-reduce.3.cloned.1.call-start = ((), (), s32[]{:S(2)}) async-start(), calls=%async_computation.2 | async-start | bytes 917504 | tf_op jit(solution)/shard_map/psum | solution.py:28
  8.4 2.7 %copy-start.3 = (f32[64,64]{1,0:T(8,128)S(1)}, f32[64,64]{1,0:T(8,128)}, u32[]{:S(2)}) copy-start(f32[64,64]{1,0:T(8,128)} %param.13) | copy-start | bytes 49156
  9.2 3.1 %copy-start.4 = (s32[4,192]{1,0:T(4,128)S(1)}, s32[4,192]{1,0:T(4,128)}, u32[]{:S(2)}) copy-start(s32[4,192]{1,0:T(4,128)} %param.10) | copy-start | bytes 9220
  9.2 3.1 %copy-start.1 = (bf16[64,512]{1,0:T(8,128)(2,1)S(1)}, bf16[64,512]{1,0:T(8,128)(2,1)}, u32[]{:S(2)}) copy-start(bf16[64,512]{1,0:T(8,128)(2,1)} %param.15) | copy-start | bytes 196612
  9.2 3.2 %copy-start.2 = (f32[64,64]{1,0:T(8,128)S(1)}, f32[64,64]{1,0:T(8,128)}, u32[]{:S(2)}) copy-start(f32[64,64]{1,0:T(8,128)} %param.14) | copy-start | bytes 49156
  12.2 245.1 %reduce-scatter.2.cloned.1.call-start = ((), (), s32[]{:S(2)}) async-start(), calls=%async_computation.1 | async-start | bytes 147456 | tf_op jit(solution)/shard_map/reduce_scatter | solution.py:52
Sparse Core Ops, SparseCore 0:
  12.3 101.0 all-reduce.2
  186.1 71.0 reduce-scatter.1
where the time goes:
time: 265 us; the launch traced here: 264 us
  waiting for transfers between devices  172 us (65%)
  blocking collectives  69.5 us (26%)
  between operations  13.5 us (5%)
  matrix products  6.97 us (3%)
    psum x1, waiting for transfers between devices, local(): in_full, out_full = lax.psum((in_part, out_part), 'hid')  100 us
    reduce_scatter x1, waiting for transfers between devices, local(): lax.psum_scatter(partial_value, 'hid', scatter_dimension=1, tiled=True)  71.2 us
    all_gather x1, blocking collectives, local(): lax.all_gather(train_feats, 'ex', axis=0, tiled=True)  69.5 us
  transfers between devices with their start and end apart: 2, of which 2 were waited for; matrix products, arithmetic and copies ran while one was open for 0% of the time, Pallas kernels for 0%

commit v1 on v0

v1 whole, which is shorter than its diff:
```python
import functools

import jax
import jax.numpy as jnp
from jax import lax
from jax.experimental import pallas as pl
from jax.experimental.pallas import tpu as pltpu
from jax.sharding import PartitionSpec as P

MESH = pl.DeviceIdType.MESH
F32 = jnp.float32
BF16 = jnp.bfloat16
SEND = jnp.float32
NT = (((1,), (1,)), ((), ()))
TN = (((0,), (0,)), ((), ()))
HIGHEST = lax.Precision.HIGHEST


def iota(shape, dim):
    return lax.broadcasted_iota(jnp.int32, shape, dim)


def kernel(
    act, grads, mask, proj_in, proj_out, inv_in, inv_out, query, out,
    act_v, grads_v, mask_v, win_v, wout_v, invin_v, invout_v, query_v,
    part, recv1, spread, qsend, qall, perm, feat, recv2, score, recv3, rows,
    in_sem, send1, got1, sendq, gotq, send2, got2, send3, got3,
):
    ex, hid = lax.axis_index("ex"), lax.axis_index("hid")
    ylo, z, core = ex // 32, (ex // 2) % 16, ex % 2
    x, yhi = hid // 2, hid % 2
    plane = (ylo * 2 + core) * 8 + hid

    def at_plane(p):
        return ((p // 16) * 32 + z * 2 + (p // 8) % 2, p % 8)

    def at_z(z2):
        return (ylo * 32 + z2 * 2 + core, hid)

    copies = []

    def load(src, dst):
        copy = pltpu.make_async_copy(src, dst, in_sem.at[len(copies)])
        copy.start()
        copies.append(copy)
        return copy

    w_loads = [load(proj_in, win_v.at[pl.ds(64 * k, 64)]) for k in range(2)]
    a_loads, g_loads = [], []
    a_loads.append(load(act.at[0], act_v.at[0]))
    for half in range(2):
        for group in range(4):
            w_loads.append(
                load(proj_out.at[pl.ds(32 * half, 32)], wout_v.at[pl.ds(128 * half + 32 * group, 32)])
            )
    g_loads.append(load(grads.at[0], grads_v.at[0]))
    for s in range(1, 4):
        a_loads.append(load(act.at[s], act_v.at[s]))
        g_loads.append(load(grads.at[s], grads_v.at[s]))
    late = [load(query, query_v), load(inv_in, invin_v), load(inv_out, invout_v), load(mask, mask_v)]

    barrier = pltpu.get_barrier_semaphore()
    for d in range(1, 32):
        pl.semaphore_signal(barrier, inc=1, device_id=at_plane((plane + d) % 32), device_id_type=MESH)
    for d in range(1, 16):
        pl.semaphore_signal(barrier, inc=1, device_id=at_z((z + d) % 16), device_id_type=MESH)

    for copy in w_loads:
        copy.wait()
    lane48 = iota((48, 128), 1)
    lane96 = iota((96, 128), 1)
    for s in range(4):
        a_loads[s].wait()
        y = lax.dot_general(act_v[s], win_v[...], NT, preferred_element_type=F32)
        packed = jnp.where(lane96 < 64, y[:96], y[96:]).astype(SEND)
        g_loads[s].wait()
        o = lax.dot_general(grads_v[s], wout_v[...], NT, preferred_element_type=F32)
        for half in range(2):
            c = o[:, 128 * half : 128 * half + 128]
            picked = jnp.where(
                lane48 < 64,
                jnp.where(lane48 < 32, c[:48], c[48:96]),
                jnp.where(lane48 < 96, c[96:144], c[144:]),
            )
            part[2 * s + half, :96] = packed
            part[2 * s + half, 96:] = picked.astype(SEND)

    pl.semaphore_wait(barrier, 46)

    def copy1(d):
        to = (hid + d) % 8
        return pltpu.make_async_remote_copy(
            part.at[to], recv1.at[d - 1], send1.at[d - 1], got1, device_id=(ex, to), device_id_type=MESH
        )

    for d in range(1, 8):
        copy1(d).start()

    for copy in late:
        copy.wait()
    m, col = iota((64, 128), 0), iota((64, 128), 1)
    place = m == 32 * (col // 64) + col % 32
    even = jnp.where(place & ((col // 32) % 2 == 0), 1.0, 0.0).astype(F32)
    odd = jnp.where(place & ((col // 32) % 2 == 1), 1.0, 0.0).astype(F32)
    both = jnp.concatenate(
        [
            jnp.dot(invout_v[...], even, precision=HIGHEST, preferred_element_type=F32),
            jnp.dot(invout_v[...], odd, precision=HIGHEST, preferred_element_type=F32),
        ],
        axis=0,
    )
    pre = [
        jnp.dot(
            query_v[:, 128 * b : 128 * b + 128].astype(F32), both, precision=HIGHEST, preferred_element_type=F32
        )
        for b in range(4)
    ]
    lane64 = iota((64, 128), 1)
    for b in range(2):
        left, right = pre[2 * b], pre[2 * b + 1]
        cols = slice(128 * b, 128 * b + 128)
        qsend[0, :, cols] = jnp.where(lane64 < 64, left, pltpu.roll(right, 64, 1)).astype(BF16)
        qsend[1, :, cols] = jnp.where(lane64 < 64, pltpu.roll(left, 64, 1), right).astype(BF16)
    my_rows = pl.ds(pl.multiple_of((ylo * 2 + core) * 64, 64), 64)

    def copyq(d):
        to = (plane + d) % 32
        return pltpu.make_async_remote_copy(
            qsend.at[to % 2], qall.at[hid, my_rows], sendq.at[d - 1], gotq, device_id=at_plane(to), device_id_type=MESH
        )

    for d in range(1, 32):
        copyq(d).start()
    pltpu.make_async_copy(qsend.at[yhi], qall.at[hid, my_rows], gotq).start()

    i, f = iota((64, 128), 0), iota((64, 128), 1)
    for k in range(16):
        pick = jnp.where(i == 4 * k + f // 32, 1.0, 0.0).astype(F32)
        spread[k] = jnp.dot(invin_v[...], pick, precision=HIGHEST, preferred_element_type=F32)
    r, c = iota((512, 256), 0), iota((512, 256), 1)
    take = (c % 16 == r // 32) & (r % 8 < 4) & (c // 16 == 4 * ((r // 8) % 4) + r % 8)
    perm[...] = jnp.where(take, 1.0, 0.0).astype(BF16)
    mask_row = mask_v[pl.ds(x, 1), :].astype(F32)
    count = jnp.sum(mask_row, axis=1, keepdims=True)
    t0, t1 = iota((48, 192), 0), iota((48, 192), 1)
    chosen = jnp.where(t1 % 48 == t0, 1.0, 0.0).astype(F32) * mask_row
    u0, u1 = iota((192, 128), 0), iota((192, 128), 1)
    group_of = jnp.where(u0 // 48 == u1 // 32, 1.0, 0.0).astype(BF16)
    weight = jnp.dot(chosen.astype(BF16), group_of, preferred_element_type=F32)

    pltpu.make_async_copy(recv1, recv1, got1).wait()
    total = part[hid].astype(F32)
    for d in range(7):
        total = total + recv1[d].astype(F32)
    side_in = total[:96]
    side_out = total[96:] * weight
    in_hi = side_in.astype(BF16)
    in_lo = (side_in - in_hi.astype(F32)).astype(BF16)
    out_hi = side_out.astype(BF16)
    out_lo = (side_out - out_hi.astype(F32)).astype(BF16)
    right = jnp.concatenate([out_hi, out_lo, out_hi], axis=0)
    first = lax.dot_general(
        jnp.concatenate([in_hi[:48], in_hi[:48], in_lo[:48]], axis=0), right, TN, preferred_element_type=F32
    )
    second = lax.dot_general(
        jnp.concatenate([in_hi[48:], in_hi[48:], in_lo[48:]], axis=0), right, TN, preferred_element_type=F32
    )
    outer = jnp.where(
        lane64 < 64,
        jnp.where(lane64 < 32, first[:64], second[:64]),
        jnp.where(lane64 < 96, first[64:], second[64:]),
    )
    outer = outer + pltpu.roll(outer, 64, 1)
    outer = outer + pltpu.roll(outer, 32, 1)
    mixed = jnp.concatenate([jnp.sum(spread[k] * outer, axis=0, keepdims=True) for k in range(16)], axis=0)
    feat[...] = (mixed / count).astype(BF16)

    def copy2(d):
        return pltpu.make_async_remote_copy(
            feat, recv2.at[z], send2.at[d - 1], got2, device_id=at_z((z + d) % 16), device_id_type=MESH
        )

    for d in range(1, 16):
        copy2(d).start()
    recv2[z] = feat[...]
    pltpu.make_async_copy(recv2.at[pl.ds(0, 15)], recv2.at[pl.ds(0, 15)], got2).wait()
    ordered = jnp.dot(perm[...], recv2[...].reshape(256, 128), preferred_element_type=F32).astype(BF16)
    total_q = jnp.zeros((32, 256), F32)
    pltpu.make_async_copy(qall, qall, gotq).wait()
    for h in range(8):
        lhs = jnp.concatenate([ordered[64 * h : 64 * h + 32], ordered[64 * h + 32 : 64 * h + 64]], axis=1)
        total_q = total_q + lax.dot_general(lhs, qall[h], NT, preferred_element_type=F32)
    score[0] = total_q[:, :128]
    score[1] = total_q[:, 128:]

    def each3(act_on):
        for block in range(4):
            for group in range(4):
                to = (block // 2 * 32 + z * 2 + block % 2, ylo * 4 + group)
                mine = (ex == to[0]) & (hid == to[1])
                src = score.at[block // 2, pl.ds(8 * group, 8)]
                act_on(src, to, mine, 4 * block + group)

    slot = core * 8 + hid

    def start3(src, to, mine, index):
        @pl.when(mine)
        def _():
            pltpu.make_async_copy(src, recv3.at[slot], got3).start()

        @pl.when(jnp.logical_not(mine))
        def _():
            pltpu.make_async_remote_copy(
                src, recv3.at[slot], send3.at[index], got3, device_id=to, device_id_type=MESH
            ).start()

    each3(start3)
    pltpu.make_async_copy(recv3, recv3, got3).wait()
    for c in range(2):
        for k in range(4):
            block = recv3[8 * c + 2 * k] + recv3[8 * c + 2 * k + 1]
            for g in range(4):
                rows[8 * g + 4 * c + k : 8 * g + 4 * c + k + 1, :] = block[g : g + 1]
    done = rows[...]
    out[...] = jnp.where(core == 0, done, pltpu.roll(done, 64, 1))[:, :64]

    for d in range(1, 8):
        copy1(d).wait_send()
    for d in range(1, 32):
        copyq(d).wait_send()
    for d in range(1, 16):
        copy2(d).wait_send()

    def end3(src, to, mine, index):
        @pl.when(jnp.logical_not(mine))
        def _():
            pltpu.make_async_remote_copy(
                src, recv3.at[slot], send3.at[index], got3, device_id=to, device_id_type=MESH
            ).wait_send()

    each3(end3)


def local(activations, out_grads, token_mask, proj_in, proj_out, inv_input, inv_output, query_feats):
    hbm = pl.BlockSpec(memory_space=pl.ANY)
    result = pl.pallas_call(
        kernel,
        out_shape=jax.ShapeDtypeStruct((32, 64), F32),
        in_specs=[hbm] * 8,
        out_specs=pl.BlockSpec(memory_space=pltpu.VMEM),
        scratch_shapes=[
            pltpu.VMEM((4, 192, 1792), BF16),
            pltpu.VMEM((4, 192, 512), BF16),
            pltpu.VMEM((4, 192), jnp.int32),
            pltpu.VMEM((128, 1792), BF16),
            pltpu.VMEM((256, 512), BF16),
            pltpu.VMEM((64, 64), F32),
            pltpu.VMEM((64, 64), F32),
            pltpu.VMEM((64, 512), BF16),
            pltpu.VMEM((8, 144, 128), SEND),
            pltpu.VMEM((7, 144, 128), SEND),
            pltpu.VMEM((16, 64, 128), F32),
            pltpu.VMEM((2, 64, 256), BF16),
            pltpu.VMEM((8, 256, 256), BF16),
            pltpu.VMEM((512, 256), BF16),
            pltpu.VMEM((16, 128), BF16),
            pltpu.VMEM((16, 16, 128), BF16),
            pltpu.VMEM((2, 32, 128), F32),
            pltpu.VMEM((16, 8, 128), F32),
            pltpu.VMEM((32, 128), F32),
            pltpu.SemaphoreType.DMA((22,)),
        ]
        + [
            pltpu.SemaphoreType.DMA((7,)),
            pltpu.SemaphoreType.DMA,
            pltpu.SemaphoreType.DMA((31,)),
            pltpu.SemaphoreType.DMA,
            pltpu.SemaphoreType.DMA((15,)),
            pltpu.SemaphoreType.DMA,
            pltpu.SemaphoreType.DMA((16,)),
            pltpu.SemaphoreType.DMA,
        ],
        compiler_params=pltpu.CompilerParams(
            collective_id=0, has_side_effects=True, vmem_limit_bytes=40 << 20
        ),
        name="scores",
    )(
        activations,
        out_grads,
        token_mask,
        proj_in.T,
        proj_out.T,
        inv_input,
        inv_output,
        query_feats,
    )
    return result.T


def solution(mesh):
    return jax.shard_map(
        local,
        mesh=mesh,
        in_specs=(
            P("ex", None, "hid"),
            P("ex", None, "hid"),
            P("ex", None),
            P("hid", None),
            P("hid", None),
            P(),
            P(),
            P("ex", "hid"),
        ),
        out_specs=P("ex", "hid"),
        check_vma=False,
    )
```

time: 265 us -> 56.5 us (0.21)
  waiting for transfers between devices: 172 us -> 0 us
  blocking collectives: 69.5 us -> 0 us
  Pallas kernels: 0 us -> 47.7 us
  between operations: 13.5 us -> 0.02 us
  matrix products: 6.97 us -> 0 us
  local copies, waits for them, and re-layouts: 2.34 us -> 8.33 us
    psum x1 -> x0, waiting for transfers between devices: 100 us -> none  [local(): in_full, out_full = lax.psum((in_part, out_part), 'hid')]
    reduce_scatter x1 -> x0, waiting for transfers between devices: 71.2 us -> none  [local(): lax.psum_scatter(partial_value, 'hid', scatter_dimension=1, tiled=True)]
    all_gather x1 -> x0, blocking collectives: 69.5 us -> none  [local(): lax.all_gather(train_feats, 'ex', axis=0, tiled=True)]
    pallas_call x0 -> x1, Pallas kernels: none -> 47.7 us  [local(): pl.pallas_call(kernel, out_shape=jax.ShapeDtypeStruct((32, 64), F32), in_...]
    unnamed x13 -> x17, local copies, waits for them, and re-layouts: 0.19 us -> 8.33 us
    dot_general x6 -> x0, matrix products: 6.97 us -> none  [the longest x1 1.92 us: local(): jnp.dot(activations.reshape(seq_count * length, unit_local), proj_in, pre...]
  transfers between devices with their start and end apart: 2 -> 0, of which waited for: 2 -> 0; matrix products, arithmetic and copies ran while one was open for 0% -> 0% of each run, Pallas kernels for 0% -> 0%
where the time goes in v1:
time: 56.5 us; the launch traced here: 56.1 us
  Pallas kernels  47.7 us (84%)
  local copies, waits for them, and re-layouts  8.33 us (15%)
    pallas_call x1, Pallas kernels, local(): pl.pallas_call(kernel, out_shape=jax.ShapeDtypeStruct((32, 64), F32), in_...  47.7 us
    unnamed x17, local copies, waits for them, and re-layouts  8.33 us

profile of v1, /device:TPU:1, one launch (start us, length us, event | category | flops | bytes accessed | tf_op | source)
XLA Modules:
  0.0 56.1 jit_solution(18016717004574898853)
XLA Ops:
  0.0 0.0 copy-start
  0.0 1.8 %copy-done = bf16[4,192,1792]{2,1,0:T(8,128)(2,1)S(1)} copy-done((bf16[4,192,1792]{2,1,0:T(8,128)(2,1)S(1)}, bf16[4,192,1792]{2,1,0:T(8,128)(2,1)}, u32[]{:S(2)}) %copy-start) | copy-done | bytes 2752536
  1.8 0.0 copy-start.1
  1.8 1.1 %copy-done.1 = bf16[4,192,512]{2,1,0:T(8,128)(2,1)S(1)} copy-done((bf16[4,192,512]{2,1,0:T(8,128)(2,1)S(1)}, bf16[4,192,512]{2,1,0:T(8,128)(2,1)}, u32[]{:S(2)}) %copy-start.1) | copy-done | bytes 786456
  2.9 0.0 copy-start.2
  2.9 0.9 %copy-done.2 = bf16[1792,64]{0,1:T(8,128)(2,1)S(1)} copy-done((bf16[1792,64]{0,1:T(8,128)(2,1)S(1)}, bf16[1792,64]{0,1:T(8,128)(2,1)}, u32[]{:S(2)}) %copy-start.2) | copy-done | bytes 229400
  3.9 0.0 copy-start.3
  3.9 0.8 %copy-done.3 = bf16[512,64]{0,1:T(8,128)(2,1)S(1)} copy-done((bf16[512,64]{0,1:T(8,128)(2,1)S(1)}, bf16[512,64]{0,1:T(8,128)(2,1)}, u32[]{:S(2)}) %copy-start.3) | copy-done | bytes 65560
  4.7 0.0 copy-start.4
  4.7 0.8 %copy-done.4 = bf16[64,512]{1,0:T(8,128)(2,1)S(1)} copy-done((bf16[64,512]{1,0:T(8,128)(2,1)S(1)}, bf16[64,512]{1,0:T(8,128)(2,1)}, u32[]{:S(2)}) %copy-start.4) | copy-done | bytes 65560
  5.5 0.0 copy-start.5
  5.5 0.8 %copy-done.5 = f32[64,64]{1,0:T(8,128)S(1)} copy-done((f32[64,64]{1,0:T(8,128)S(1)}, f32[64,64]{1,0:T(8,128)}, u32[]{:S(2)}) %copy-start.5) | copy-done | bytes 16408
  6.3 0.0 copy-start.6
  6.3 0.8 %copy-done.6 = f32[64,64]{1,0:T(8,128)S(1)} copy-done((f32[64,64]{1,0:T(8,128)S(1)}, f32[64,64]{1,0:T(8,128)}, u32[]{:S(2)}) %copy-start.6) | copy-done | bytes 16408
  7.0 0.0 copy-start.7
  7.0 0.7 %copy-done.7 = s32[4,192]{1,0:T(4,128)S(1)} copy-done((s32[4,192]{1,0:T(4,128)S(1)}, s32[4,192]{1,0:T(4,128)}, u32[]{:S(2)}) %copy-start.7) | copy-done | bytes 3096
  7.7 47.7 %scores.1 = f32[32,64]{1,0:T(8,128)S(1)} custom-call(bf16[4,192,1792]{2,1,0:T(8,128)(2,1)S(1)} %copy-done, bf16[4,192,512]{2,1,0:T(8,128)(2,1)S(1)} %copy-done.1, s32[4,192]{1,0:T(4,128)S(1)} %copy-done.7, bf16[64,1792]{1,0:T(8,128)(2,1)S(1)} %bitcast.3, bf16[64,512]{1,0:T(8,128)(2,1)S(1)} %bitcast.4, f32[64,64]{1,0:T(8,128)S(1)} %copy-done.5, ...), custom_call_target="tpu_custom_call" | custom-call | tf_op jit(solution)/shard_map/scores/pallas_call | solution.py:246
  55.5 0.6 %copy.10 = f32[64,32]{0,1:T(8,128)} copy(f32[64,32]{0,1:T(8,128)S(1)} %bitcast.5) | data formatting | bytes 16384
Async XLA Ops:
  0.0 1.8 %copy-start = (bf16[4,192,1792]{2,1,0:T(8,128)(2,1)S(1)}, bf16[4,192,1792]{2,1,0:T(8,128)(2,1)}, u32[]{:S(2)}) copy-start(bf16[4,192,1792]{2,1,0:T(8,128)(2,1)} %act.1) | copy-start | bytes 8257540
  1.8 1.1 %copy-start.1 = (bf16[4,192,512]{2,1,0:T(8,128)(2,1)S(1)}, bf16[4,192,512]{2,1,0:T(8,128)(2,1)}, u32[]{:S(2)}) copy-start(bf16[4,192,512]{2,1,0:T(8,128)(2,1)} %grads.1) | copy-start | bytes 2359300
  2.9 0.9 %copy-start.2 = (bf16[1792,64]{0,1:T(8,128)(2,1)S(1)}, bf16[1792,64]{0,1:T(8,128)(2,1)}, u32[]{:S(2)}) copy-start(bf16[1792,64]{0,1:T(8,128)(2,1)} %param.11) | copy-start | bytes 688132
  3.9 0.8 %copy-start.3 = (bf16[512,64]{0,1:T(8,128)(2,1)S(1)}, bf16[512,64]{0,1:T(8,128)(2,1)}, u32[]{:S(2)}) copy-start(bf16[512,64]{0,1:T(8,128)(2,1)} %param.12) | copy-start | bytes 196612
  4.7 0.8 %copy-start.4 = (bf16[64,512]{1,0:T(8,128)(2,1)S(1)}, bf16[64,512]{1,0:T(8,128)(2,1)}, u32[]{:S(2)}) copy-start(bf16[64,512]{1,0:T(8,128)(2,1)} %query.1) | copy-start | bytes 196612
  5.5 0.8 %copy-start.5 = (f32[64,64]{1,0:T(8,128)S(1)}, f32[64,64]{1,0:T(8,128)}, u32[]{:S(2)}) copy-start(f32[64,64]{1,0:T(8,128)} %inv_in.1) | copy-start | bytes 49156
  6.3 0.8 %copy-start.6 = (f32[64,64]{1,0:T(8,128)S(1)}, f32[64,64]{1,0:T(8,128)}, u32[]{:S(2)}) copy-start(f32[64,64]{1,0:T(8,128)} %inv_out.1) | copy-start | bytes 49156
  7.0 0.7 %copy-start.7 = (s32[4,192]{1,0:T(4,128)S(1)}, s32[4,192]{1,0:T(4,128)}, u32[]{:S(2)}) copy-start(s32[4,192]{1,0:T(4,128)} %mask.1) | copy-start | bytes 9220

commit v2 on v1

v2 whole, which is shorter than its diff:
```python
import functools

import jax
import jax.numpy as jnp
from jax import lax
from jax.experimental import pallas as pl
from jax.experimental.pallas import tpu as pltpu
from jax.sharding import PartitionSpec as P

MESH = pl.DeviceIdType.MESH
F32 = jnp.float32
BF16 = jnp.bfloat16
SEND = jnp.float32
NT = (((1,), (1,)), ((), ()))
TN = (((0,), (0,)), ((), ()))
HIGHEST = lax.Precision.HIGHEST


def iota(shape, dim):
    return lax.broadcasted_iota(jnp.int32, shape, dim)


def kernel(
    act, grads, mask, proj_in, proj_out, inv_in, inv_out, query, out,
    act_v, grads_v, mask_v, win_v, wout_v, invin_v, invout_v, query_v,
    part, recv1, spread, qsend, qall, perm, feat, recv2,
    in_sem, send1, got1, sendq, gotq, send2, got2, send3, got3, met1, met2,
):
    ex, hid = lax.axis_index("ex"), lax.axis_index("hid")
    ylo, z, core = ex // 32, (ex // 2) % 16, ex % 2
    x, yhi = hid // 2, hid % 2

    def near(dy, dz):
        return (((ylo + dy) % 2) * 32 + ((z + dz + 16) % 16) * 2 + core, hid)

    def tell(sem, to):
        pl.semaphore_signal(sem, inc=1, device_id=to, device_id_type=MESH)

    other = (ex + 1 - 2 * core, hid)

    copies = []

    def load(src, dst):
        copy = pltpu.make_async_copy(src, dst, in_sem.at[len(copies)])
        copy.start()
        copies.append(copy)
        return copy

    loads = [load(proj_in, win_v.at[pl.ds(64 * k, 64)]) for k in range(2)]
    for half in range(2):
        for group in range(4):
            loads.append(
                load(proj_out.at[pl.ds(32 * half, 32)], wout_v.at[pl.ds(128 * half + 32 * group, 32)])
            )
    stages = []
    for s in range(4):
        stages.append([load(act.at[s], act_v.at[s]), load(grads.at[s], grads_v.at[s])])
    late = [load(query, query_v), load(inv_in, invin_v), load(inv_out, invout_v), load(mask, mask_v)]

    barrier = pltpu.get_barrier_semaphore()
    for d in range(1, 8):
        tell(barrier, (ex, (hid + d) % 8))
    tell(barrier, other)
    tell(barrier, near(1, 0))
    for d in (-4, -3, -2, -1, 1, 2, 3, 4):
        tell(barrier, near(0, d))

    for copy in loads:
        copy.wait()
    lane48 = iota((48, 128), 1)
    lane96 = iota((96, 128), 1)
    for stage in ((0, 1), (2, 3)):
        for s in stage:
            for copy in stages[s]:
                copy.wait()
        for s in stage:
            y = lax.dot_general(act_v[s], win_v[...], NT, preferred_element_type=F32)
            packed = jnp.where(lane96 < 64, y[:96], y[96:]).astype(SEND)
            o = lax.dot_general(grads_v[s], wout_v[...], NT, preferred_element_type=F32)
            for half in range(2):
                c = o[:, 128 * half : 128 * half + 128]
                picked = jnp.where(
                    lane48 < 64,
                    jnp.where(lane48 < 32, c[:48], c[48:96]),
                    jnp.where(lane48 < 96, c[96:144], c[144:]),
                )
                part[2 * s + half, :96] = packed
                part[2 * s + half, 96:] = picked.astype(SEND)

    pl.semaphore_wait(barrier, 17)

    def copy1(d):
        to = (hid + d) % 8
        return pltpu.make_async_remote_copy(
            part.at[to], recv1.at[d - 1], send1.at[d - 1], got1, device_id=(ex, to), device_id_type=MESH
        )

    for d in range(1, 8):
        copy1(d).start()
    for d in (-4, -3, -2, -1, 1, 2, 3, 4):
        tell(met1, near(0, d))

    for copy in late:
        copy.wait()
    m, col = iota((64, 128), 0), iota((64, 128), 1)
    place = m == 32 * (col // 64) + col % 32
    even = jnp.where(place & ((col // 32) % 2 == 0), 1.0, 0.0).astype(F32)
    odd = jnp.where(place & ((col // 32) % 2 == 1), 1.0, 0.0).astype(F32)
    both = jnp.concatenate(
        [
            jnp.dot(invout_v[...], even, precision=HIGHEST, preferred_element_type=F32),
            jnp.dot(invout_v[...], odd, precision=HIGHEST, preferred_element_type=F32),
        ],
        axis=0,
    )
    pre = [
        jnp.dot(
            query_v[:, 128 * b : 128 * b + 128].astype(F32), both, precision=HIGHEST, preferred_element_type=F32
        )
        for b in range(4)
    ]
    lane64 = iota((64, 128), 1)
    for b in range(2):
        left, right = pre[2 * b], pre[2 * b + 1]
        qsend[:, 128 * b : 128 * b + 128] = jnp.where(lane64 < 64, left, pltpu.roll(right, 64, 1)).astype(BF16)
        qsend[:, 256 + 128 * b : 384 + 128 * b] = jnp.where(
            lane64 < 64, pltpu.roll(left, 64, 1), right
        ).astype(BF16)
    qall[hid] = qsend[...]

    def copyq(d):
        return pltpu.make_async_remote_copy(
            qsend, qall.at[hid], sendq.at[d - 1], gotq, device_id=(ex, (hid + d) % 8), device_id_type=MESH
        )

    pl.semaphore_wait(met1, 8)
    for dy in range(2):
        for dz in (-4, 4):
            tell(met2, near(dy, dz))

    i, f = iota((64, 128), 0), iota((64, 128), 1)
    for k in range(16):
        pick = jnp.where(i == 4 * k + f // 32, 1.0, 0.0).astype(F32)
        spread[k] = jnp.dot(invin_v[...], pick, precision=HIGHEST, preferred_element_type=F32)
    r, c = iota((256, 256), 0), iota((256, 256), 1)
    perm[...] = jnp.where((c % 16 == r // 16) & (c // 16 == r % 16), 1.0, 0.0).astype(BF16)
    mask_row = mask_v[pl.ds(x, 1), :].astype(F32)
    count = jnp.sum(mask_row, axis=1, keepdims=True)
    t0, t1 = iota((48, 192), 0), iota((48, 192), 1)
    chosen = jnp.where(t1 % 48 == t0, 1.0, 0.0).astype(F32) * mask_row
    u0, u1 = iota((192, 128), 0), iota((192, 128), 1)
    group_of = jnp.where(u0 // 48 == u1 // 32, 1.0, 0.0).astype(BF16)
    weight = jnp.dot(chosen.astype(BF16), group_of, preferred_element_type=F32)
    pl.semaphore_wait(met2, 4)

    pltpu.make_async_copy(recv1, recv1, got1).wait()
    total = part[hid].astype(F32)
    for d in range(7):
        total = total + recv1[d].astype(F32)
    side_in = total[:96]
    side_out = total[96:] * weight
    in_hi = side_in.astype(BF16)
    in_lo = (side_in - in_hi.astype(F32)).astype(BF16)
    out_hi = side_out.astype(BF16)
    out_lo = (side_out - out_hi.astype(F32)).astype(BF16)
    right = jnp.concatenate([out_hi, out_lo, out_hi], axis=0)
    first = lax.dot_general(
        jnp.concatenate([in_hi[:48], in_hi[:48], in_lo[:48]], axis=0), right, TN, preferred_element_type=F32
    )
    second = lax.dot_general(
        jnp.concatenate([in_hi[48:], in_hi[48:], in_lo[48:]], axis=0), right, TN, preferred_element_type=F32
    )
    outer = jnp.where(
        lane64 < 64,
        jnp.where(lane64 < 32, first[:64], second[:64]),
        jnp.where(lane64 < 96, first[64:], second[64:]),
    )
    outer = outer + pltpu.roll(outer, 64, 1)
    outer = outer + pltpu.roll(outer, 32, 1)
    mixed = jnp.concatenate([jnp.sum(spread[k] * outer, axis=0, keepdims=True) for k in range(16)], axis=0)
    feat[...] = (mixed / count).astype(BF16)

    home = ex // 8
    slot = (z % 4) * 4 + x
    order = [(dy, dz) for dz in (8, 7, 9, 6, 10, 5, 11, 4, 12, 3, 13, 2, 14, 1, 15, 0) for dy in (1, 0)]

    def copy2(n):
        return pltpu.make_async_remote_copy(
            feat, recv2.at[0, yhi, slot], send2.at[n], got2,
            device_id=(near(*order[n])[0], home), device_id_type=MESH,
        )

    for n in range(31):
        copy2(n).start()

    @pl.when(hid != home)
    def _():
        copy2(31).start()

    @pl.when(hid == home)
    def _():
        pltpu.make_async_copy(feat, recv2.at[0, yhi, slot], got2).start()

    for d in range(1, 8):
        copyq(d).start()

    for d in range(1, 8):
        copy1(d).wait_send()
    for n in range(31):
        copy2(n).wait_send()

    @pl.when(hid != home)
    def _():
        copy2(31).wait_send()

    for d in range(1, 8):
        copyq(d).wait_send()
    pltpu.make_async_copy(qall.at[pl.ds(0, 7)], qall.at[pl.ds(0, 7)], gotq).wait()
    pltpu.make_async_copy(recv2.at[0], recv2.at[0], got2).wait()

    copy3 = pltpu.make_async_remote_copy(
        recv2.at[0], recv2.at[1], send3, got3, device_id=other, device_id_type=MESH
    )
    copy3.start()
    queries = jnp.concatenate([qall[h] for h in range(8)], axis=1)

    def scores(side):
        ordered = [
            jnp.dot(perm[...], recv2[side, half].reshape(256, 128), preferred_element_type=F32).astype(BF16)
            for half in range(2)
        ]
        lhs = jnp.concatenate(
            [
                ordered[half][32 * h + 16 * k : 32 * h + 16 * k + 16]
                for h in range(8)
                for half in range(2)
                for k in range(2)
            ],
            axis=1,
        )
        return lax.dot_general(lhs, queries, NT, preferred_element_type=F32)

    mine = scores(0)
    copy3.wait()
    theirs = scores(1)
    even = jnp.where(core == 0, mine, theirs)
    odd = jnp.where(core == 0, theirs, mine)
    for g in range(4):
        out[8 * g : 8 * g + 4, :] = even[4 * g : 4 * g + 4]
        out[8 * g + 4 : 8 * g + 8, :] = odd[4 * g : 4 * g + 4]


def local(activations, out_grads, token_mask, proj_in, proj_out, inv_input, inv_output, query_feats):
    hbm = pl.BlockSpec(memory_space=pltpu.HBM)
    result = pl.pallas_call(
        kernel,
        out_shape=jax.ShapeDtypeStruct((32, 64), F32),
        in_specs=[hbm] * 8,
        out_specs=pl.BlockSpec(memory_space=pltpu.VMEM),
        scratch_shapes=[
            pltpu.VMEM((4, 192, 1792), BF16),
            pltpu.VMEM((4, 192, 512), BF16),
            pltpu.VMEM((4, 192), jnp.int32),
            pltpu.VMEM((128, 1792), BF16),
            pltpu.VMEM((256, 512), BF16),
            pltpu.VMEM((64, 64), F32),
            pltpu.VMEM((64, 64), F32),
            pltpu.VMEM((64, 512), BF16),
            pltpu.VMEM((8, 144, 128), SEND),
            pltpu.VMEM((7, 144, 128), SEND),
            pltpu.VMEM((16, 64, 128), F32),
            pltpu.VMEM((64, 512), BF16),
            pltpu.VMEM((8, 64, 512), BF16),
            pltpu.VMEM((256, 256), BF16),
            pltpu.VMEM((16, 128), BF16),
            pltpu.VMEM((2, 2, 16, 16, 128), BF16),
            pltpu.SemaphoreType.DMA((22,)),
            pltpu.SemaphoreType.DMA((7,)),
            pltpu.SemaphoreType.DMA,
            pltpu.SemaphoreType.DMA((7,)),
            pltpu.SemaphoreType.DMA,
            pltpu.SemaphoreType.DMA((32,)),
            pltpu.SemaphoreType.DMA,
            pltpu.SemaphoreType.DMA,
            pltpu.SemaphoreType.DMA,
            pltpu.SemaphoreType.REGULAR,
            pltpu.SemaphoreType.REGULAR,
        ],
        compiler_params=pltpu.CompilerParams(
            collective_id=0, has_side_effects=True, vmem_limit_bytes=66_000_000
        ),
        name="scores",
    )(
        activations,
        out_grads,
        token_mask,
        proj_in.T,
        proj_out.T,
        inv_input,
        inv_output,
        query_feats,
    )
    return result.T


def solution(mesh):
    return jax.shard_map(
        local,
        mesh=mesh,
        in_specs=(
            P("ex", None, "hid"),
            P("ex", None, "hid"),
            P("ex", None),
            P("hid", None),
            P("hid", None),
            P(),
            P(),
            P("ex", "hid"),
        ),
        out_specs=P("ex", "hid"),
        check_vma=False,
    )
```

time: 56.5 us -> 40.3 us (0.71)
  the two profiles are of different devices: /device:TPU:1 before, /device:TPU:3 now
where the time goes in v2:
time: 40.3 us; the launch traced here: 40.1 us
  Pallas kernels  38.8 us (96%)
  local copies, waits for them, and re-layouts  1.32 us (3%)
    pallas_call x1, Pallas kernels, local(): pl.pallas_call(kernel, out_shape=jax.ShapeDtypeStruct((32, 64), F32), in_...  38.8 us
    unnamed x1, local copies, waits for them, and re-layouts  1.32 us

profile of v2, /device:TPU:3, one launch (start us, length us, event | category | flops | bytes accessed | tf_op | source)
XLA Modules:
  0.0 40.1 jit_solution(13587905026861851185)
XLA Ops:
  0.0 38.8 %scores.1 = f32[32,64]{1,0:T(8,128)} custom-call(bf16[4,192,1792]{2,1,0:T(8,128)(2,1)} %act.1, bf16[4,192,512]{2,1,0:T(8,128)(2,1)} %grads.1, s32[4,192]{1,0:T(4,128)} %mask.1, bf16[64,1792]{1,0:T(8,128)(2,1)} %bitcast.3, bf16[64,512]{1,0:T(8,128)(2,1)} %bitcast.4, f32[64,64]{1,0:T(8,128)} %inv_in.1, f32[64,64]{1,0:T(8,128)} %inv_out.1, bf16[64,512]{1,0:T(8,128)(2,1)} %query.1), custom_call_target="tpu_custom_call" | custom-call | tf_op jit(solution)/shard_map/scores/pallas_call | solution.py:255
  38.8 1.3 %copy.10 = f32[64,32]{0,1:T(8,128)} copy(f32[64,32]{0,1:T(8,128)} %bitcast.5) | data formatting | bytes 16384

commit v3 on v2

--- a/solution.py
+++ b/solution.py
@@ -10,7 +10,7 @@
 MESH = pl.DeviceIdType.MESH
 F32 = jnp.float32
 BF16 = jnp.bfloat16
-SEND = jnp.float32
+IN_SENT, OUT_SENT = BF16, F32
 NT = (((1,), (1,)), ((), ()))
 TN = (((0,), (0,)), ((), ()))
 HIGHEST = lax.Precision.HIGHEST
@@ -23,8 +23,8 @@
 def kernel(
     act, grads, mask, proj_in, proj_out, inv_in, inv_out, query, out,
     act_v, grads_v, mask_v, win_v, wout_v, invin_v, invout_v, query_v,
-    part, recv1, spread, qsend, qall, perm, feat, recv2,
-    in_sem, send1, got1, sendq, gotq, send2, got2, send3, got3, met1, met2,
+    part_in, part_out, own_in, own_out, from_in, from_out, spread, qsend, qall, perm, feat, recv2,
+    in_sem, send1_in, send1_out, got1_in, got1_out, sendq, gotq, send2, got2, send3, got3, met1, met2,
 ):
     ex, hid = lax.axis_index("ex"), lax.axis_index("hid")
     ylo, z, core = ex // 32, (ex // 2) % 16, ex % 2
@@ -46,57 +46,76 @@
         copies.append(copy)
         return copy
 
+    def sequence(step):
+        s = (x + step) % 4
+        return [load(act.at[s], act_v.at[step]), load(grads.at[s], grads_v.at[step])]
+
     loads = [load(proj_in, win_v.at[pl.ds(64 * k, 64)]) for k in range(2)]
+    first = sequence(2)
     for half in range(2):
         for group in range(4):
             loads.append(
                 load(proj_out.at[pl.ds(32 * half, 32)], wout_v.at[pl.ds(128 * half + 32 * group, 32)])
             )
-    stages = []
-    for s in range(4):
-        stages.append([load(act.at[s], act_v.at[s]), load(grads.at[s], grads_v.at[s])])
-    late = [load(query, query_v), load(inv_in, invin_v), load(inv_out, invout_v), load(mask, mask_v)]
 
     barrier = pltpu.get_barrier_semaphore()
     for d in range(1, 8):
         tell(barrier, (ex, (hid + d) % 8))
+    for d in (-4, -3, -2, -1, 1, 2, 3, 4):
+        tell(barrier, near(0, d))
     tell(barrier, other)
     tell(barrier, near(1, 0))
-    for d in (-4, -3, -2, -1, 1, 2, 3, 4):
-        tell(barrier, near(0, d))
-
-    for copy in loads:
-        copy.wait()
+    rest = [copy for step in (1, 3, 0) for copy in sequence(step)]
+    late = [load(query, query_v), load(inv_in, invin_v), load(inv_out, invout_v), load(mask, mask_v)]
+
     lane48 = iota((48, 128), 1)
     lane96 = iota((96, 128), 1)
-    for stage in ((0, 1), (2, 3)):
-        for s in stage:
-            for copy in stages[s]:
-                copy.wait()
-        for s in stage:
-            y = lax.dot_general(act_v[s], win_v[...], NT, preferred_element_type=F32)
-            packed = jnp.where(lane96 < 64, y[:96], y[96:]).astype(SEND)
-            o = lax.dot_general(grads_v[s], wout_v[...], NT, preferred_element_type=F32)
-            for half in range(2):
-                c = o[:, 128 * half : 128 * half + 128]
-                picked = jnp.where(
-                    lane48 < 64,
-                    jnp.where(lane48 < 32, c[:48], c[48:96]),
-                    jnp.where(lane48 < 96, c[96:144], c[144:]),
-                )
-                part[2 * s + half, :96] = packed
-                part[2 * s + half, 96:] = picked.astype(SEND)
-
+
+    def project(step):
+        y = lax.dot_general(act_v[step], win_v[...], NT, preferred_element_type=F32)
+        packed = jnp.where(lane96 < 64, y[:96], y[96:])
+        part_in[step] = packed.astype(IN_SENT)
+        o = lax.dot_general(grads_v[step], wout_v[...], NT, preferred_element_type=F32)
+        if step == 0:
+            own_in[...] = packed
+        for half in range(2):
+            c = o[:, 128 * half : 128 * half + 128]
+            picked = jnp.where(
+                lane48 < 64,
+                jnp.where(lane48 < 32, c[:48], c[48:96]),
+                jnp.where(lane48 < 96, c[96:144], c[144:]),
+            )
+            part_out[step, half] = picked.astype(OUT_SENT)
+            if step == 0:
+                own_out[half] = picked
+
+    def copy1(n):
+        step, half = ((2, 0), (2, 1), (1, 0), (1, 1), (3, 0), (3, 1), (0, 1 - yhi))[n]
+        to = ((x + step) % 4) * 2 + half
+        at = (to - hid + 8) % 8 - 1
+        return [
+            pltpu.make_async_remote_copy(
+                part_in.at[step], from_in.at[at], send1_in.at[n], got1_in, device_id=(ex, to), device_id_type=MESH
+            ),
+            pltpu.make_async_remote_copy(
+                part_out.at[step, half], from_out.at[at], send1_out.at[n], got1_out,
+                device_id=(ex, to), device_id_type=MESH,
+            ),
+        ]
+
+    def start1(messages):
+        for n in messages:
+            for copy in copy1(n):
+                copy.start()
+
+    for copy in loads + first:
+        copy.wait()
+    for copy in rest:
+        copy.wait()
+    for step in (2, 1, 3, 0):
+        project(step)
     pl.semaphore_wait(barrier, 17)
-
-    def copy1(d):
-        to = (hid + d) % 8
-        return pltpu.make_async_remote_copy(
-            part.at[to], recv1.at[d - 1], send1.at[d - 1], got1, device_id=(ex, to), device_id_type=MESH
-        )
-
-    for d in range(1, 8):
-        copy1(d).start()
+    start1(range(7))
     for d in (-4, -3, -2, -1, 1, 2, 3, 4):
         tell(met1, near(0, d))
 
@@ -153,12 +172,13 @@
     weight = jnp.dot(chosen.astype(BF16), group_of, preferred_element_type=F32)
     pl.semaphore_wait(met2, 4)
 
-    pltpu.make_async_copy(recv1, recv1, got1).wait()
-    total = part[hid].astype(F32)
-    for d in range(7):
-        total = total + recv1[d].astype(F32)
-    side_in = total[:96]
-    side_out = total[96:] * weight
+    pltpu.make_async_copy(from_out, from_out, got1_out).wait()
+    pltpu.make_async_copy(from_in, from_in, got1_in).wait()
+    side_in, side_out = own_in[...], own_out[yhi]
+    for n in range(7):
+        side_in = side_in + from_in[n].astype(F32)
+        side_out = side_out + from_out[n].astype(F32)
+    side_out = side_out * weight
     in_hi = side_in.astype(BF16)
     in_lo = (side_in - in_hi.astype(F32)).astype(BF16)
     out_hi = side_out.astype(BF16)
@@ -204,8 +224,9 @@
     for d in range(1, 8):
         copyq(d).start()
 
-    for d in range(1, 8):
-        copy1(d).wait_send()
+    for n in range(7):
+        for copy in copy1(n):
+            copy.wait_send()
     for n in range(31):
         copy2(n).wait_send()
 
@@ -266,8 +287,12 @@
             pltpu.VMEM((64, 64), F32),
             pltpu.VMEM((64, 64), F32),
             pltpu.VMEM((64, 512), BF16),
-            pltpu.VMEM((8, 144, 128), SEND),
-            pltpu.VMEM((7, 144, 128), SEND),
+            pltpu.VMEM((4, 96, 128), IN_SENT),
+            pltpu.VMEM((4, 2, 48, 128), OUT_SENT),
+            pltpu.VMEM((96, 128), F32),
+            pltpu.VMEM((2, 48, 128), F32),
+            pltpu.VMEM((7, 96, 128), IN_SENT),
+            pltpu.VMEM((7, 48, 128), OUT_SENT),
             pltpu.VMEM((16, 64, 128), F32),
             pltpu.VMEM((64, 512), BF16),
             pltpu.VMEM((8, 64, 512), BF16),
@@ -276,6 +301,8 @@
             pltpu.VMEM((2, 2, 16, 16, 128), BF16),
             pltpu.SemaphoreType.DMA((22,)),
             pltpu.SemaphoreType.DMA((7,)),
+            pltpu.SemaphoreType.DMA((7,)),
+            pltpu.SemaphoreType.DMA,
             pltpu.SemaphoreType.DMA,
             pltpu.SemaphoreType.DMA((7,)),
             pltpu.SemaphoreType.DMA,
@@ -287,18 +314,23 @@
             pltpu.SemaphoreType.REGULAR,
         ],
         compiler_params=pltpu.CompilerParams(
-            collective_id=0, has_side_effects=True, vmem_limit_bytes=66_000_000
+            collective_id=0, has_side_effects=True, vmem_limit_bytes=40 << 20
         ),
         name="scores",
     )(
-        activations,
-        out_grads,
-        token_mask,
-        proj_in.T,
-        proj_out.T,
-        inv_input,
-        inv_output,
-        query_feats,
+        *(
+            pltpu.with_memory_space_constraint(array, pltpu.HBM)
+            for array in (
+                activations,
+                out_grads,
+                token_mask,
+                proj_in.T,
+                proj_out.T,
+                inv_input,
+                inv_output,
+                query_feats,
+            )
+        )
     )
     return result.T
 

time: 40.3 us -> 37.7 us (0.935)
  the two profiles are of different devices: /device:TPU:3 before, /device:TPU:1 now
where the time goes in v3:
time: 37.7 us; the launch traced here: 37.6 us
  Pallas kernels  37 us (98%)
  local copies, waits for them, and re-layouts  0.61 us (2%)
    pallas_call x1, Pallas kernels, local(): pl.pallas_call(kernel, out_shape=jax.ShapeDtypeStruct((32, 64), F32), in_...  37 us

profile of v3, /device:TPU:1, one launch (start us, length us, event | category | flops | bytes accessed | tf_op | source)
XLA Modules:
  0.0 37.6 jit_solution(3351952153245297031)
XLA Ops:
  0.0 37.0 %scores.1 = f32[32,64]{1,0:T(8,128)S(1)} custom-call(bf16[4,192,1792]{2,1,0:T(8,128)(2,1)} %act.1, bf16[4,192,512]{2,1,0:T(8,128)(2,1)} %grads.1, s32[4,192]{1,0:T(4,128)} %mask.1, bf16[64,1792]{1,0:T(8,128)(2,1)} %bitcast.4, bf16[64,512]{1,0:T(8,128)(2,1)} %bitcast.5, f32[64,64]{1,0:T(8,128)} %inv_in.1, f32[64,64]{1,0:T(8,128)} %inv_out.1, ...), custom_call_target="tpu_custom_call" | custom-call | tf_op jit(solution)/shard_map/scores/pallas_call | solution.py:276
  37.0 0.6 %copy.10 = f32[64,32]{0,1:T(8,128)} copy(f32[64,32]{0,1:T(8,128)S(1)} %bitcast.3) | data formatting | bytes 16384

commit v4 on v3

--- a/solution.py
+++ b/solution.py
@@ -50,13 +50,10 @@
         s = (x + step) % 4
         return [load(act.at[s], act_v.at[step]), load(grads.at[s], grads_v.at[step])]
 
-    loads = [load(proj_in, win_v.at[pl.ds(64 * k, 64)]) for k in range(2)]
-    first = sequence(2)
-    for half in range(2):
-        for group in range(4):
-            loads.append(
-                load(proj_out.at[pl.ds(32 * half, 32)], wout_v.at[pl.ds(128 * half + 32 * group, 32)])
-            )
+    late = [load(inv_in, invin_v), load(inv_out, invout_v), load(query, query_v), load(mask, mask_v)]
+    first = [copy for step in (2, 1) for copy in sequence(step)]
+    loads = [load(proj_in, win_v), load(proj_out, wout_v)]
+    rest = [copy for step in (3, 0) for copy in sequence(step)]
 
     barrier = pltpu.get_barrier_semaphore()
     for d in range(1, 8):
@@ -65,17 +62,16 @@
         tell(barrier, near(0, d))
     tell(barrier, other)
     tell(barrier, near(1, 0))
-    rest = [copy for step in (1, 3, 0) for copy in sequence(step)]
-    late = [load(query, query_v), load(inv_in, invin_v), load(inv_out, invout_v), load(mask, mask_v)]
-
     lane48 = iota((48, 128), 1)
     lane96 = iota((96, 128), 1)
 
     def project(step):
-        y = lax.dot_general(act_v[step], win_v[...], NT, preferred_element_type=F32)
+        win = jnp.concatenate([win_v[...]] * 2, axis=0)
+        wout = jnp.concatenate([wout_v[:32]] * 4 + [wout_v[32:]] * 4, axis=0)
+        y = lax.dot_general(act_v[step], win, NT, preferred_element_type=F32)
         packed = jnp.where(lane96 < 64, y[:96], y[96:])
         part_in[step] = packed.astype(IN_SENT)
-        o = lax.dot_general(grads_v[step], wout_v[...], NT, preferred_element_type=F32)
+        o = lax.dot_general(grads_v[step], wout, NT, preferred_element_type=F32)
         if step == 0:
             own_in[...] = packed
         for half in range(2):
@@ -110,31 +106,41 @@
 
     for copy in loads + first:
         copy.wait()
+    for step in (2, 1):
+        project(step)
+    pl.semaphore_wait(barrier, 17)
+    start1((0, 1, 2, 3))
+    for d in (-4, -3, -2, -1, 1, 2, 3, 4):
+        tell(met1, near(0, d))
     for copy in rest:
         copy.wait()
-    for step in (2, 1, 3, 0):
+    for step in (3, 0):
         project(step)
-    pl.semaphore_wait(barrier, 17)
-    start1(range(7))
-    for d in (-4, -3, -2, -1, 1, 2, 3, 4):
-        tell(met1, near(0, d))
+    start1((4, 5, 6))
+
+    def exact3(array):
+        high = array.astype(BF16)
+        left = array - high.astype(F32)
+        middle = left.astype(BF16)
+        return high, middle, (left - middle.astype(F32)).astype(BF16)
 
     for copy in late:
         copy.wait()
     m, col = iota((64, 128), 0), iota((64, 128), 1)
     place = m == 32 * (col // 64) + col % 32
-    even = jnp.where(place & ((col // 32) % 2 == 0), 1.0, 0.0).astype(F32)
-    odd = jnp.where(place & ((col // 32) % 2 == 1), 1.0, 0.0).astype(F32)
+    even = jnp.where(place & ((col // 32) % 2 == 0), 1.0, 0.0).astype(BF16)
+    odd = jnp.where(place & ((col // 32) % 2 == 1), 1.0, 0.0).astype(BF16)
     both = jnp.concatenate(
         [
-            jnp.dot(invout_v[...], even, precision=HIGHEST, preferred_element_type=F32),
-            jnp.dot(invout_v[...], odd, precision=HIGHEST, preferred_element_type=F32),
+            jnp.dot(piece, where_to, preferred_element_type=F32).astype(BF16)
+            for piece in exact3(invout_v[...])
+            for where_to in (even, odd)
         ],
         axis=0,
     )
     pre = [
         jnp.dot(
-            query_v[:, 128 * b : 128 * b + 128].astype(F32), both, precision=HIGHEST, preferred_element_type=F32
+            jnp.concatenate([query_v[:, 128 * b : 128 * b + 128]] * 3, axis=1), both, preferred_element_type=F32
         )
         for b in range(4)
     ]
@@ -147,20 +153,16 @@
         ).astype(BF16)
     qall[hid] = qsend[...]
 
-    def copyq(d):
-        return pltpu.make_async_remote_copy(
-            qsend, qall.at[hid], sendq.at[d - 1], gotq, device_id=(ex, (hid + d) % 8), device_id_type=MESH
-        )
-
     pl.semaphore_wait(met1, 8)
     for dy in range(2):
         for dz in (-4, 4):
             tell(met2, near(dy, dz))
 
     i, f = iota((64, 128), 0), iota((64, 128), 1)
+    pieces = jnp.concatenate(exact3(invin_v[...]), axis=1)
     for k in range(16):
-        pick = jnp.where(i == 4 * k + f // 32, 1.0, 0.0).astype(F32)
-        spread[k] = jnp.dot(invin_v[...], pick, precision=HIGHEST, preferred_element_type=F32)
+        pick = jnp.where(i == 4 * k + f // 32, 1.0, 0.0).astype(BF16)
+        spread[k] = jnp.dot(pieces, jnp.concatenate([pick] * 3, axis=0), preferred_element_type=F32)
     r, c = iota((256, 256), 0), iota((256, 256), 1)
     perm[...] = jnp.where((c % 16 == r // 16) & (c // 16 == r % 16), 1.0, 0.0).astype(BF16)
     mask_row = mask_v[pl.ds(x, 1), :].astype(F32)
@@ -170,6 +172,12 @@
     u0, u1 = iota((192, 128), 0), iota((192, 128), 1)
     group_of = jnp.where(u0 // 48 == u1 // 32, 1.0, 0.0).astype(BF16)
     weight = jnp.dot(chosen.astype(BF16), group_of, preferred_element_type=F32)
+
+    def copyq(d):
+        return pltpu.make_async_remote_copy(
+            qsend, qall.at[hid], sendq.at[d - 1], gotq, device_id=(ex, (hid + d) % 8), device_id_type=MESH
+        )
+
     pl.semaphore_wait(met2, 4)
 
     pltpu.make_async_copy(from_out, from_out, got1_out).wait()
@@ -282,8 +290,8 @@
             pltpu.VMEM((4, 192, 1792), BF16),
             pltpu.VMEM((4, 192, 512), BF16),
             pltpu.VMEM((4, 192), jnp.int32),
-            pltpu.VMEM((128, 1792), BF16),
-            pltpu.VMEM((256, 512), BF16),
+            pltpu.VMEM((64, 1792), BF16),
+            pltpu.VMEM((64, 512), BF16),
             pltpu.VMEM((64, 64), F32),
             pltpu.VMEM((64, 64), F32),
             pltpu.VMEM((64, 512), BF16),
@@ -299,7 +307,7 @@
             pltpu.VMEM((256, 256), BF16),
             pltpu.VMEM((16, 128), BF16),
             pltpu.VMEM((2, 2, 16, 16, 128), BF16),
-            pltpu.SemaphoreType.DMA((22,)),
+            pltpu.SemaphoreType.DMA((14,)),
             pltpu.SemaphoreType.DMA((7,)),
             pltpu.SemaphoreType.DMA((7,)),
             pltpu.SemaphoreType.DMA,

time: 37.7 us -> 36.4 us (0.966)
  Pallas kernels: 37 us -> 35.6 us
    pallas_call x1, Pallas kernels: 37 us -> 35.6 us  [local(): pl.pallas_call(kernel, out_shape=jax.ShapeDtypeStruct((32, 64), F32), in_...]
where the time goes in v4:
time: 36.4 us; the launch traced here: 36.3 us
  Pallas kernels  35.6 us (98%)
  local copies, waits for them, and re-layouts  0.61 us (2%)
    pallas_call x1, Pallas kernels, local(): pl.pallas_call(kernel, out_shape=jax.ShapeDtypeStruct((32, 64), F32), in_...  35.6 us

profile of v4, /device:TPU:1, one launch (start us, length us, event | category | flops | bytes accessed | tf_op | source)
XLA Modules:
  0.0 36.3 jit_solution(16877978495411208466)
XLA Ops:
  0.0 35.6 %scores.1 = f32[32,64]{1,0:T(8,128)S(1)} custom-call(bf16[4,192,1792]{2,1,0:T(8,128)(2,1)} %act.1, bf16[4,192,512]{2,1,0:T(8,128)(2,1)} %grads.1, s32[4,192]{1,0:T(4,128)} %mask.1, bf16[64,1792]{1,0:T(8,128)(2,1)} %bitcast.4, bf16[64,512]{1,0:T(8,128)(2,1)} %bitcast.5, f32[64,64]{1,0:T(8,128)} %inv_in.1, f32[64,64]{1,0:T(8,128)} %inv_out.1, ...), custom_call_target="tpu_custom_call" | custom-call | tf_op jit(solution)/shard_map/scores/pallas_call | solution.py:284
  35.6 0.6 %copy.10 = f32[64,32]{0,1:T(8,128)} copy(f32[64,32]{0,1:T(8,128)S(1)} %bitcast.3) | data formatting | bytes 16384

commit v5 on v4

--- a/solution.py
+++ b/solution.py
@@ -10,7 +10,7 @@
 MESH = pl.DeviceIdType.MESH
 F32 = jnp.float32
 BF16 = jnp.bfloat16
-IN_SENT, OUT_SENT = BF16, F32
+IN_SENT, OUT_SENT = BF16, BF16
 NT = (((1,), (1,)), ((), ()))
 TN = (((0,), (0,)), ((), ()))
 HIGHEST = lax.Precision.HIGHEST
@@ -178,7 +178,6 @@
             qsend, qall.at[hid], sendq.at[d - 1], gotq, device_id=(ex, (hid + d) % 8), device_id_type=MESH
         )
 
-    pl.semaphore_wait(met2, 4)
 
     pltpu.make_async_copy(from_out, from_out, got1_out).wait()
     pltpu.make_async_copy(from_in, from_in, got1_in).wait()
@@ -210,7 +209,8 @@
 
     home = ex // 8
     slot = (z % 4) * 4 + x
-    order = [(dy, dz) for dz in (8, 7, 9, 6, 10, 5, 11, 4, 12, 3, 13, 2, 14, 1, 15, 0) for dy in (1, 0)]
+    early = [(0, dz) for dz in (4, 12, 3, 13, 2, 14, 1, 15)]
+    order = early + [(dy, dz) for dz in (8, 7, 9, 6, 10, 5, 11, 4, 12, 3, 13, 2, 14, 1, 15, 0) for dy in (1, 0) if (dy, dz) not in early and (dy, dz) != (0, 0)] + [(0, 0)]
 
     def copy2(n):
         return pltpu.make_async_remote_copy(
@@ -218,7 +218,10 @@
             device_id=(near(*order[n])[0], home), device_id_type=MESH,
         )
 
-    for n in range(31):
+    for n in range(len(early)):
+        copy2(n).start()
+    pl.semaphore_wait(met2, 4)
+    for n in range(len(early), 31):
         copy2(n).start()
 
     @pl.when(hid != home)

time: 36.4 us -> 35.6 us (0.978)
  Pallas kernels: 35.6 us -> 34.9 us
    pallas_call x1, Pallas kernels: 35.6 us -> 34.9 us  [local(): pl.pallas_call(kernel, out_shape=jax.ShapeDtypeStruct((32, 64), F32), in_...]
where the time goes in v5:
time: 35.6 us; the launch traced here: 35.5 us
  Pallas kernels  34.9 us (98%)
  local copies, waits for them, and re-layouts  0.61 us (2%)
    pallas_call x1, Pallas kernels, local(): pl.pallas_call(kernel, out_shape=jax.ShapeDtypeStruct((32, 64), F32), in_...  34.9 us

profile of v5, /device:TPU:1, one launch (start us, length us, event | category | flops | bytes accessed | tf_op | source)
XLA Modules:
  0.0 35.5 jit_solution(4857613471976826941)
XLA Ops:
  0.0 34.9 %scores.1 = f32[32,64]{1,0:T(8,128)S(1)} custom-call(bf16[4,192,1792]{2,1,0:T(8,128)(2,1)} %act.1, bf16[4,192,512]{2,1,0:T(8,128)(2,1)} %grads.1, s32[4,192]{1,0:T(4,128)} %mask.1, bf16[64,1792]{1,0:T(8,128)(2,1)} %bitcast.4, bf16[64,512]{1,0:T(8,128)(2,1)} %bitcast.5, f32[64,64]{1,0:T(8,128)} %inv_in.1, f32[64,64]{1,0:T(8,128)} %inv_out.1, ...), custom_call_target="tpu_custom_call" | custom-call | tf_op jit(solution)/shard_map/scores/pallas_call | solution.py:287
  34.9 0.6 %copy.10 = f32[64,32]{0,1:T(8,128)} copy(f32[64,32]{0,1:T(8,128)S(1)} %bitcast.3) | data formatting | bytes 16384

commit v6 on v5

--- a/solution.py
+++ b/solution.py
@@ -50,10 +50,8 @@
         s = (x + step) % 4
         return [load(act.at[s], act_v.at[step]), load(grads.at[s], grads_v.at[step])]
 
-    late = [load(inv_in, invin_v), load(inv_out, invout_v), load(query, query_v), load(mask, mask_v)]
     first = [copy for step in (2, 1) for copy in sequence(step)]
     loads = [load(proj_in, win_v), load(proj_out, wout_v)]
-    rest = [copy for step in (3, 0) for copy in sequence(step)]
 
     barrier = pltpu.get_barrier_semaphore()
     for d in range(1, 8):
@@ -62,6 +60,9 @@
         tell(barrier, near(0, d))
     tell(barrier, other)
     tell(barrier, near(1, 0))
+    rest = [copy for step in (3, 0) for copy in sequence(step)]
+    late = [load(inv_in, invin_v), load(inv_out, invout_v), load(query, query_v), load(mask, mask_v)]
+
     lane48 = iota((48, 128), 1)
     lane96 = iota((96, 128), 1)
 
@@ -109,9 +110,9 @@
     for step in (2, 1):
         project(step)
     pl.semaphore_wait(barrier, 17)
-    start1((0, 1, 2, 3))
     for d in (-4, -3, -2, -1, 1, 2, 3, 4):
         tell(met1, near(0, d))
+    start1((0, 1, 2, 3))
     for copy in rest:
         copy.wait()
     for step in (3, 0):
@@ -247,13 +248,13 @@
 
     for d in range(1, 8):
         copyq(d).wait_send()
-    pltpu.make_async_copy(qall.at[pl.ds(0, 7)], qall.at[pl.ds(0, 7)], gotq).wait()
     pltpu.make_async_copy(recv2.at[0], recv2.at[0], got2).wait()
 
     copy3 = pltpu.make_async_remote_copy(
         recv2.at[0], recv2.at[1], send3, got3, device_id=other, device_id_type=MESH
     )
     copy3.start()
+    pltpu.make_async_copy(qall.at[pl.ds(0, 7)], qall.at[pl.ds(0, 7)], gotq).wait()
     queries = jnp.concatenate([qall[h] for h in range(8)], axis=1)
 
     def scores(side):

time: 35.6 us -> 35.4 us (level)
  the two profiles are of different devices: /device:TPU:1 before, /device:TPU:3 now
where the time goes in v6:
time: 35.4 us; the launch traced here: 35.3 us
  Pallas kernels  34.7 us (98%)
  local copies, waits for them, and re-layouts  0.61 us (2%)
    pallas_call x1, Pallas kernels, local(): pl.pallas_call(kernel, out_shape=jax.ShapeDtypeStruct((32, 64), F32), in_...  34.7 us

profile of v6, /device:TPU:3, one launch (start us, length us, event | category | flops | bytes accessed | tf_op | source)
XLA Modules:
  0.0 35.3 jit_solution(6885419880855523860)
XLA Ops:
  0.0 34.7 %scores.1 = f32[32,64]{1,0:T(8,128)S(1)} custom-call(bf16[4,192,1792]{2,1,0:T(8,128)(2,1)} %act.1, bf16[4,192,512]{2,1,0:T(8,128)(2,1)} %grads.1, s32[4,192]{1,0:T(4,128)} %mask.1, bf16[64,1792]{1,0:T(8,128)(2,1)} %bitcast.4, bf16[64,512]{1,0:T(8,128)(2,1)} %bitcast.5, f32[64,64]{1,0:T(8,128)} %inv_in.1, f32[64,64]{1,0:T(8,128)} %inv_out.1, ...), custom_call_target="tpu_custom_call" | custom-call | tf_op jit(solution)/shard_map/scores/pallas_call | solution.py:288
  34.7 0.6 %copy.10 = f32[64,32]{0,1:T(8,128)} copy(f32[64,32]{0,1:T(8,128)S(1)} %bitcast.3) | data formatting | bytes 16384

commit v7 on v6

--- a/solution.py
+++ b/solution.py
@@ -236,18 +236,6 @@
     for d in range(1, 8):
         copyq(d).start()
 
-    for n in range(7):
-        for copy in copy1(n):
-            copy.wait_send()
-    for n in range(31):
-        copy2(n).wait_send()
-
-    @pl.when(hid != home)
-    def _():
-        copy2(31).wait_send()
-
-    for d in range(1, 8):
-        copyq(d).wait_send()
     pltpu.make_async_copy(recv2.at[0], recv2.at[0], got2).wait()
 
     copy3 = pltpu.make_async_remote_copy(
@@ -281,6 +269,19 @@
     for g in range(4):
         out[8 * g : 8 * g + 4, :] = even[4 * g : 4 * g + 4]
         out[8 * g + 4 : 8 * g + 8, :] = odd[4 * g : 4 * g + 4]
+
+    for n in range(7):
+        for copy in copy1(n):
+            copy.wait_send()
+    for n in range(31):
+        copy2(n).wait_send()
+
+    @pl.when(hid != home)
+    def _():
+        copy2(31).wait_send()
+
+    for d in range(1, 8):
+        copyq(d).wait_send()
 
 
 def local(activations, out_grads, token_mask, proj_in, proj_out, inv_input, inv_output, query_feats):

time: 35.4 us -> 35.5 us (level)
  no operation moved by 1% of the time
where the time goes in v7:
time: 35.5 us; the launch traced here: 35.4 us
  Pallas kernels  34.8 us (98%)
  local copies, waits for them, and re-layouts  0.61 us (2%)
    pallas_call x1, Pallas kernels, local(): pl.pallas_call(kernel, out_shape=jax.ShapeDtypeStruct((32, 64), F32), in_...  34.8 us

profile of v7, /device:TPU:3, one launch (start us, length us, event | category | flops | bytes accessed | tf_op | source)
XLA Modules:
  0.0 35.4 jit_solution(2671065628139199695)
XLA Ops:
  0.0 34.8 %scores.1 = f32[32,64]{1,0:T(8,128)S(1)} custom-call(bf16[4,192,1792]{2,1,0:T(8,128)(2,1)} %act.1, bf16[4,192,512]{2,1,0:T(8,128)(2,1)} %grads.1, s32[4,192]{1,0:T(4,128)} %mask.1, bf16[64,1792]{1,0:T(8,128)(2,1)} %bitcast.4, bf16[64,512]{1,0:T(8,128)(2,1)} %bitcast.5, f32[64,64]{1,0:T(8,128)} %inv_in.1, f32[64,64]{1,0:T(8,128)} %inv_out.1, ...), custom_call_target="tpu_custom_call" | custom-call | tf_op jit(solution)/shard_map/scores/pallas_call | solution.py:289
  34.8 0.6 %copy.10 = f32[64,32]{0,1:T(8,128)} copy(f32[64,32]{0,1:T(8,128)S(1)} %bitcast.3) | data formatting | bytes 16384
